TPU v7x, 256 devices: a whole 4x4x8 slice. The times are simulated.
256 devices in a mesh: row: 64 (over x, z_lo, y, core), col: 4 (over z_hi).
Axes of the slice: x: 4, y: 4, z: 8 (z_hi: 4, z_lo: 2; z = z_hi * 2 + z_lo), core: 2. Of those that a mesh axis runs over, the one named last changes fastest.
Arguments:
- fields: float32 [4, 128, 512, 512], P(None, 'row', None, 'col'), may hold values from -6 to 6
- diffusivity: float32 [4], replicated, may hold values from 0.05 to 0.3
- records: float32 [6, 2097152], P(None, ('row', 'col')), may hold values from -6 to 6
- response_time: float32 [2097152], P(('row', 'col')), may hold values from 0.5 to 4
- cell_index: int32 [2097152], P(('row', 'col')), may hold values from 0 to 131071
- counts: int32 [256], P(('row', 'col')), may hold values from 4096 to 8192, as said below
- destination: int32 [2097152], P(('row', 'col')), may hold values from 0 to 4, as said below
- slot: int32 [2097152], P(('row', 'col')), may hold values from 0 to 255, as said below
Outputs:
- tendency: float32 [4, 128, 512, 512], P(None, 'row', None, 'col')
- kept: float32 [6, 2097152], P(None, ('row', 'col'))
- arrivals: float32 [4, 6, 65536], P(None, None, ('row', 'col'))
Inputs may be any that keep to these rules, and one draw needn't show every extreme that they name: `counts`: both wall rows of pencils are full. `destination`: only live particles leave; none leaves row index 0 downward or row index 63 upward. For each pencil and direction the leaving particles' slots are distinct; pencil 0 sends exactly 256 particles toward col index + 1; slot is 0 for particles that stay.
All inputs are finite; a program needn't handle non-finite values.
Results may differ from a plain program's by a relative error of at most 0.00009.
Values sent between devices are 32-bit elements; how exact they have to be, the bound alone decides.
A program may use at most 192 MiB of HBM per device.

v0:
```python
import math
import jax
import jax.numpy as jnp
from jax import lax
from jax.sharding import PartitionSpec as P

PART_DEV = 8192
MIG = 256
time_step = 0.2
coupling = 0.5
stretch = 1.5


def shifted(value, axis, steps):
    count = lax.axis_size(axis)
    first, last = (max(0, -steps), min(count, count - steps))
    return lax.ppermute(value, axis, [(source, source + steps) for source in range(first, last)])


def from_behind(block, axis, distance):
    devices = range(lax.axis_size(axis))
    route = [((i - distance) % len(devices), i) for i in devices]
    return lax.ppermute(block, axis, route)


def periodic_compact(points):
    index = jnp.arange(points, dtype=jnp.int32)
    offset = (index[None, :] - index[:, None]) % points
    lhs = jnp.where(offset == 0, 1.0, 0.0) + jnp.where(
        (offset == 1) | (offset == points - 1), 1.0 / 3.0, 0.0
    )
    rhs = jnp.where(offset == 1, 7.0 / 9.0, 0.0) - jnp.where(offset == points - 1, 7.0 / 9.0, 0.0)
    rhs = (
        rhs
        + jnp.where(offset == 2, 1.0 / 36.0, 0.0)
        - jnp.where(offset == points - 2, 1.0 / 36.0, 0.0)
    )
    factor = jnp.linalg.cholesky(lhs.astype(jnp.float32))
    return jax.scipy.linalg.cho_solve((factor, True), rhs.astype(jnp.float32))


def wall_compact(points):
    index = jnp.arange(points, dtype=jnp.int32)
    first = index == 0
    final = index == points - 1
    near = (index == 1) | (index == points - 2)
    lower = jnp.where(first, 0.0, jnp.where(final, 2.0, jnp.where(near, 0.25, 1.0 / 3.0))).astype(
        jnp.float32
    )
    upper = jnp.where(final, 0.0, jnp.where(first, 2.0, jnp.where(near, 0.25, 1.0 / 3.0))).astype(
        jnp.float32
    )
    middle = jnp.ones((points,), jnp.float32)
    offset = index[None, :] - index[:, None]
    inner = jnp.where(offset == 1, 7.0 / 9.0, 0.0) - jnp.where(offset == -1, 7.0 / 9.0, 0.0)
    inner = (
        inner + jnp.where(offset == 2, 1.0 / 36.0, 0.0) - jnp.where(offset == -2, 1.0 / 36.0, 0.0)
    )
    padde_rows = jnp.where(offset == 1, 0.75, 0.0) - jnp.where(offset == -1, 0.75, 0.0)
    top_row = (
        jnp.where(offset == 0, -2.5, 0.0)
        + jnp.where(offset == 1, 2.0, 0.0)
        + jnp.where(offset == 2, 0.5, 0.0)
    )
    end_row = (
        jnp.where(offset == 0, 2.5, 0.0)
        - jnp.where(offset == -1, 2.0, 0.0)
        - jnp.where(offset == -2, 0.5, 0.0)
    )
    rhs = jnp.where(
        first[:, None],
        top_row,
        jnp.where(final[:, None], end_row, jnp.where(near[:, None], padde_rows, inner)),
    )
    solved = lax.linalg.tridiagonal_solve(lower, middle, upper, rhs.astype(jnp.float32))
    coord = -1.0 + 2.0 * index.astype(jnp.float32) / (points - 1)
    slope = stretch * (1.0 - jnp.tanh(stretch * coord) ** 2) / math.tanh(stretch)
    return solved / slope[:, None]


def spectral_matrix(points):
    index = jnp.arange(points, dtype=jnp.int32)
    offset = index[:, None] - index[None, :]
    parity = (1 - 2 * (offset % 2)).astype(jnp.float32)
    angle = math.pi * offset.astype(jnp.float32) / points
    safe_angle = jnp.where(offset == 0, 1.0, angle)
    value = math.pi / points * parity * jnp.cos(safe_angle) / jnp.sin(safe_angle)
    return jnp.where(offset == 0, 0.0, value)


def spanwise_terms(pencil_data, viscous):
    highest = lax.Precision.HIGHEST
    deriv_z = spectral_matrix(pencil_data.shape[3])
    second_z = jnp.dot(deriv_z, deriv_z, precision=highest)
    along_z = jnp.einsum("ij,cabj->cabi", deriv_z, pencil_data, precision=highest)
    curve_z = jnp.einsum("ij,cabj->cabi", second_z, pencil_data, precision=highest)
    return -pencil_data[2] * along_z + viscous * curve_z


def on_device(fields, diffusivity, records, response_time, cell_index, counts, destination, slot):
    highest = lax.Precision.HIGHEST
    viscous = diffusivity[:, None, None, None]
    planes = fields.shape[2]
    deriv_x = periodic_compact(planes)
    second_x = jnp.dot(deriv_x, deriv_x, precision=highest)
    along_x = jnp.einsum("ij,cyjz->cyiz", deriv_x, fields, precision=highest)
    curve_x = jnp.einsum("ij,cyjz->cyiz", second_x, fields, precision=highest)
    partial_x = -fields[0] * along_x + viscous * curve_x
    local = jnp.arange(PART_DEV, dtype=jnp.int32)
    live = local < counts[0]
    flat_speed = fields[0:3].reshape(3, -1)
    fluid = jnp.take(flat_speed, cell_index, axis=1)
    drag = (fluid - records[3:6]) / response_time
    velocity = records[3:6] + time_step * drag
    moved_pos = records[0:3] + time_step * velocity
    moved = jnp.concatenate([moved_pos, velocity], axis=0)
    force = jnp.where(live[None, :], -coupling * drag, 0.0)
    deposit = (
        jnp.zeros_like(flat_speed)
        .at[:, cell_index]
        .add(force)
        .reshape(3, fields.shape[1], fields.shape[2], fields.shape[3])
    )
    partial_x = partial_x.at[0:3].add(deposit)
    normal_pencil = lax.all_to_all(fields, "row", split_axis=2, concat_axis=1, tiled=True)
    deriv_y = wall_compact(normal_pencil.shape[1])
    second_y = jnp.dot(deriv_y, deriv_y, precision=highest)
    along_y = jnp.einsum("ij,cjxz->cixz", deriv_y, normal_pencil, precision=highest)
    curve_y = jnp.einsum("ij,cjxz->cixz", second_y, normal_pencil, precision=highest)
    partial_y = -normal_pencil[1] * along_y + viscous * curve_y
    span_pencil = lax.all_to_all(normal_pencil, "col", split_axis=1, concat_axis=3, tiled=True)
    partial_z = spanwise_terms(span_pencil, viscous)
    partial_y = partial_y + lax.all_to_all(
        partial_z, "col", split_axis=3, concat_axis=1, tiled=True
    )
    tendency = partial_x + lax.all_to_all(partial_y, "row", split_axis=1, concat_axis=2, tiled=True)
    staying = live & (destination == 0)
    kept = jnp.where(staying[None, :], moved, 0.0)
    leaving = live & (destination > 0)
    target = jnp.where(leaving, (destination - 1) * MIG + slot, 4 * MIG)
    outgoing = (
        jnp.zeros((6, 4 * MIG + 1), jnp.float32)
        .at[:, target]
        .add(jnp.where(leaving[None, :], moved, 0.0))
    )
    outgoing = outgoing[:, : 4 * MIG].reshape(6, 4, MIG)
    received = []
    for direction, offset in ((0, 1), (1, -1)):
        received.append(shifted(outgoing[:, direction], "row", offset))
    for direction, offset in ((2, 1), (3, -1)):
        received.append(from_behind(outgoing[:, direction], "col", offset))
    arrivals = jnp.stack(received, axis=0)
    return (tendency, kept, arrivals)


def solution(mesh):
    return jax.shard_map(
        on_device,
        mesh=mesh,
        in_specs=(
            P(None, "row", None, "col"),
            P(),
            P(None, ("row", "col")),
            P(("row", "col")),
            P(("row", "col")),
            P(("row", "col")),
            P(("row", "col")),
            P(("row", "col")),
        ),
        out_specs=(
            P(None, "row", None, "col"),
            P(None, ("row", "col")),
            P(None, None, ("row", "col")),
        ),
        check_vma=False,
    )
```

profile of v0, /device:TPU:1, one launch (start us, length us, event | category | flops | bytes accessed | tf_op | source)
XLA Modules:
  0.0 1095.8 jit_solution(8864007310958328743)
XLA Ops:
  0.6 4.3 copy.115
  4.9 10.5 all-to-all-start
  16.9 30.5 %copy.111 = f32[3,2,512,128]{0,3,2,1:T(8,128)} copy(f32[3,2,512,128]{3,2,1,0:T(8,128)S(1)} %slice-done) | data formatting | bytes 3145728 | tf_op jit(solution)/shard_map/slice | solution.py:111
  47.3 118.4 %gather_fusion = f32[8192,3]{1,0:T(8,128)} fusion(f32[3,131072]{0,1:T(8,128)} %bitcast.277, s32[8192]{0:T(1024)S(1)} %get-tuple-element.480), kind=kCustom, calls=%fused_computation | custom fusion | bytes 229376 | tf_op jit(solution)/shard_map/jit(_take)/gather | solution.py:112
  165.7 2.9 copy.112
  170.3 2.7 copy.126
  173.0 53.6 %scatter_custom_fusion.1 = f32[6,1025]{0,1:T(8,128)S(1)} fusion(s32[8192]{0:T(1024)S(1)} %compare_select_fusion, f32[8192,6]{1,0:T(8,128)} %copy.126, f32[]{:T(128)} %constant.319.clone.1), kind=kCustom, calls=%fused_computation.317 | custom fusion | flops 49152 | bytes 25112 | tf_op jit(solution)/shard_map/scatter-add | solution.py:144
  226.8 4.2 collective-permute-start.3
  232.4 5.2 collective-permute-start.1
  242.7 194.9 %while.34 = (s32[]{:T(128)}, f32[]{:T(128)}, f32[128]{0:T(128)S(1)}, f32[3,32]{1,0:T(4,128)S(1)}, f32[3,32,128]{2,1,0:T(8,128)S(1)}, /*index=5*/f32[3,32]{1,0:T(...) while((s32[]{:T(128)}, f32[]{:T(128)}, ...), condition=%wide.region_10.11_spmd, body=%wide.region_9.10_spmd.sunk | while | flops 12417 | bytes 103669 | solution.py:75
  286.5 20.2 %fusion.526 = (f32[128]{0:T(128)S(1)}, f32[128]{0:T(128)S(1)}, f32[128]{0:T(128)S(1)}, f32[128]{0:T(128)S(1)}, f32[128]{0:T(128)S(1)}, /*index=5*/f32[128]{0:T(1...) fusion(f32[3,32,128]{2,1,0:T(8,128)S(1)} %get-tuple-element.112, ...), kind=kLoop, calls=%fused_computation.44.clone.1 | loop fusion | flops 12288 | bytes 33664 | tf_op jit(solution)/shard_map/while/body/eval_jaxpr/div | solution.py:75
  351.4 20.2 %fusion.526 = (f32[128]{0:T(128)S(1)}, f32[128]{0:T(128)S(1)}, f32[128]{0:T(128)S(1)}, f32[128]{0:T(128)S(1)}, f32[128]{0:T(128)S(1)}, /*index=5*/f32[128]{0:T(1...) fusion(f32[3,32,128]{2,1,0:T(8,128)S(1)} %get-tuple-element.112, ...), kind=kLoop, calls=%fused_computation.44.clone.1 | loop fusion | flops 12288 | bytes 33664 | tf_op jit(solution)/shard_map/while/body/eval_jaxpr/div | solution.py:75
  416.2 20.2 %fusion.526 = (f32[128]{0:T(128)S(1)}, f32[128]{0:T(128)S(1)}, f32[128]{0:T(128)S(1)}, f32[128]{0:T(128)S(1)}, f32[128]{0:T(128)S(1)}, /*index=5*/f32[128]{0:T(1...) fusion(f32[3,32,128]{2,1,0:T(8,128)S(1)} %get-tuple-element.112, ...), kind=kLoop, calls=%fused_computation.44.clone.1 | loop fusion | flops 12288 | bytes 33664 | tf_op jit(solution)/shard_map/while/body/eval_jaxpr/div | solution.py:75
  441.4 11.7 %cholesky.104 = f32[128,128]{1,0:T(8,128)S(1)} custom-call(f32[128,128]{1,0:T(8,128)S(1)} %cholesky.266), custom_call_target="Cholesky" | custom-call | tf_op jit(solution)/shard_map/jit(cholesky)/cholesky | solution.py:38
  453.3 9.8 custom-call.34
  463.7 11.7 %cholesky.217 = f32[128,128]{1,0:T(8,128)S(1)} custom-call(f32[128,128]{1,0:T(8,128)S(1)} %cholesky.270), custom_call_target="Cholesky" | custom-call | tf_op jit(solution)/shard_map/jit(cholesky)/cholesky | solution.py:38
  475.5 10.0 custom-call.35
  486.1 11.7 %cholesky.238 = f32[128,128]{1,0:T(8,128)S(1)} custom-call(f32[128,128]{1,0:T(8,128)S(1)} %cholesky.275), custom_call_target="Cholesky" | custom-call | tf_op jit(solution)/shard_map/jit(cholesky)/cholesky | solution.py:38
  497.9 9.8 custom-call.36
  508.3 11.7 %cholesky.255 = f32[128,128]{1,0:T(8,128)S(1)} custom-call(f32[128,128]{1,0:T(8,128)S(1)} %convolution_subtract_fusion.8), custom_call_target="Cholesky" | custom-call | tf_op jit(solution)/shard_map/jit(cholesky)/cholesky | solution.py:38
  560.4 19.7 %fusion.304 = (f32[128]{0:T(128)S(1)}, f32[128]{0:T(128)S(1)}, f32[128]{0:T(128)S(1)}, f32[128]{0:T(128)S(1)}, f32[128]{0:T(128)S(1)}, /*index=5*/f32[128]{0:T(1...) fusion(f32[128,128]{1,0:T(8,128)S(1)} %select_select_fusion.1, ...), kind=kLoop, calls=%fused_computation.488 | loop fusion | flops 11904 | bytes 32504 | tf_op jit(solution)/shard_map/eval_jaxpr/div | solution.py:75
  584.4 6.5 sort
  591.0 65.7 %while.35 = (s32[]{:T(128)}, f32[128]{0:T(128)S(1)}, f32[3,32,128]{2,1,0:T(8,128)S(1)}, f32[3,32,128]{2,1,0:T(8,128)S(1)}, f32[3,32]{1,0:T(4,128)S(1)}, /*index=...) while((s32[]{:T(128)}, f32[128]{0:T(128)S(1)}, ...), condition=%wide.region_12.13_spmd, body=%wide.region_11.12_spmd.sunk | while | flops 8226 | bytes 101341 | solution.py:75
  592.4 20.3 %fusion.529 = (f32[128]{0:T(128)S(1)}, f32[128]{0:T(128)S(1)}, f32[128]{0:T(128)S(1)}, f32[128]{0:T(128)S(1)}, f32[128]{0:T(128)S(1)}, /*index=5*/f32[128]{0:T(1...) fusion(f32[3,32,128]{2,1,0:T(8,128)S(1)} %get-tuple-element.123, ...), kind=kLoop, calls=%fused_computation.172.clone.1 | loop fusion | flops 8192 | bytes 33536 | tf_op jit(solution)/shard_map/while/body/eval_jaxpr/sub | solution.py:75
  614.3 20.3 %fusion.529 = (f32[128]{0:T(128)S(1)}, f32[128]{0:T(128)S(1)}, f32[128]{0:T(128)S(1)}, f32[128]{0:T(128)S(1)}, f32[128]{0:T(128)S(1)}, /*index=5*/f32[128]{0:T(1...) fusion(f32[3,32,128]{2,1,0:T(8,128)S(1)} %get-tuple-element.123, ...), kind=kLoop, calls=%fused_computation.172.clone.1 | loop fusion | flops 8192 | bytes 33536 | tf_op jit(solution)/shard_map/while/body/eval_jaxpr/sub | solution.py:75
  636.2 20.3 %fusion.529 = (f32[128]{0:T(128)S(1)}, f32[128]{0:T(128)S(1)}, f32[128]{0:T(128)S(1)}, f32[128]{0:T(128)S(1)}, f32[128]{0:T(128)S(1)}, /*index=5*/f32[128]{0:T(1...) fusion(f32[3,32,128]{2,1,0:T(8,128)S(1)} %get-tuple-element.123, ...), kind=kLoop, calls=%fused_computation.172.clone.1 | loop fusion | flops 8192 | bytes 33536 | tf_op jit(solution)/shard_map/while/body/eval_jaxpr/sub | solution.py:75
  658.4 3.3 fusion.368
  661.7 3.3 fusion.367
  665.0 3.2 fusion.366
  668.2 3.1 fusion.365
  671.3 3.1 fusion.364
  674.5 3.1 fusion.363
  677.5 3.2 fusion.362
  680.8 3.3 fusion.361
  684.1 7.0 convolution_bitcast_fusion
  691.2 2.7 copy.148
  696.4 5.4 all-to-all-start.1
  701.9 10.2 while.36
  712.2 38.1 %all-to-all-done.1 = f32[4,128,8,128]{3,2,0,1:T(8,128)} async-done(((f32[4,128,8,128]{3,2,0,1:T(8,128)}), f32[4,128,8,128]{3,2,0,1:T(8,128)}, u32[]{:S(2)}, u32[]{:S(2)}) %all-to-all-start.1) | async-done | bytes 2097184 | tf_op jit(solution)/shard_map/all_to_all | solution.py:131
  750.3 4.3 copy.121
  754.6 3.1 all_to_all.59
  761.0 3.5 fusion.493
  764.6 9.0 bitcast_add_fusion.2
  773.6 8.4 copy.122
  782.0 7.3 reshape.572
  789.3 4.5 all-to-all-start.2
  793.8 2.7 fusion.360
  796.4 40.7 %custom-call.37 = f32[4,128,128]{1,2,0:T(8,128)} custom-call(f32[4,128,128]{2,1,0:T(8,128)} %get-tuple-element.177), custom_call_target="InvertDiagBlocksLowerTriangular" | custom-call | tf_op jit(solution)/shard_map/jit(_cho_solve)/triangular_solve | solution.py:39
  837.2 2.7 copy.113
  839.8 121.9 %scatter_custom_fusion = f32[3,131072]{0,1:T(8,128)} fusion(s32[8192]{0:T(1024)} %get-tuple-element.196, f32[]{:T(128)} %constant.319.clone.1, f32[8192,3]{1,0:T(8,128)} %copy.113, s32[8192]{0:T(1024)S(1)} %broadcast_clamp_fusion), kind=kCustom, calls=%fused_computation.235 | custom fusion | flops 24576 | bytes 1573376 | tf_op jit(solution)/shard_map/scatter-add | solution.py:121
  961.8 36.1 %copy.138 = f32[3,2,512,128]{3,2,1,0:T(8,128)} copy(f32[3,2,512,128]{0,3,2,1:T(8,128)} %bitcast.280) | data formatting | bytes 3145728 | tf_op jit(solution)/shard_map/reshape.84
  1000.6 2.6 fusion.358
  1003.2 2.7 fusion.357
  1005.9 2.7 fusion.356
  1018.8 3.2 fusion.226
  1022.6 9.0 reduce.26
  1031.5 7.8 reshape.573
  1039.3 6.3 copy.123
  1045.6 4.5 bitcast_add_fusion.1
  1052.6 11.0 %all-to-all-start.3 = ((f32[4,128,8,128]{3,2,0,1:T(8,128)}), f32[4,128,8,128]{3,2,0,1:T(8,128)}, u32[]{:S(2)}, u32[]{:S(2)}) async-start(f32[4,128,8,128]{3,2,0,1:T(8,128)} %copy.124), calls=%async_computation.3 | async-start | bytes 4194304 | tf_op jit(solution)/shard_map/all_to_all | solution.py:136
  1070.6 3.6 fusion.492
  1074.2 3.7 bitcast_add_fusion.3
  1079.7 12.5 %all-to-all-done.3 = f32[4,128,8,128]{3,2,0,1:T(8,128)} async-done(((f32[4,128,8,128]{3,2,0,1:T(8,128)}), f32[4,128,8,128]{3,2,0,1:T(8,128)}, u32[]{:S(2)}, u32[]{:S(2)}) %all-to-all-start.3) | async-done | bytes 2097184 | tf_op jit(solution)/shard_map/all_to_all | solution.py:136
  1092.3 3.1 bitcast_add_fusion
  (216 shorter events, 74.4 us)
Async XLA Ops:
  4.9 686.3 %all-to-all-start = ((f32[4,2,512,128]{3,0,1,2:T(4,128)}), f32[4,2,512,128]{3,0,1,2:T(4,128)}, u32[]{:S(2)}, u32[]{:S(2)}) async-start(f32[4,2,512,128]{3,0,1,2:T(4,128)} %copy.115), calls=%async_computation | async-start | bytes 4194304 | tf_op jit(solution)/shard_map/all_to_all | solution.py:125
  15.4 0.8 copy-start.10
  15.4 1.4 slice-start
  165.7 3.6 copy-start.11
  165.7 3.6 copy-start.9
  165.7 3.6 copy-start.12
  170.3 2.7 copy-start.13
  226.8 851.6 %collective-permute-start.3 = (f32[6,256]{1,0:T(8,128)S(1)}, f32[6,256]{1,0:T(8,128)}, u32[]{:S(2)}, u32[]{:S(2)}) collective-permute-start(f32[6,256]{1,0:T(8,128)S(1)} %bitcast.1864), channel_id=1, source_target_pairs={{1,0},{2,1},{3,2},{0,3},{5,4},{6,5},{7,6},{4,7},{9,8},{10,9},{11,1... | collective-permute-start | bytes 18440 | tf_op jit(solution)/shard_map/ppermute | solution.py:23
  231.7 846.7 %collective-permute-start.2 = (f32[6,256]{1,0:T(8,128)}, f32[6,256]{1,0:T(8,128)}, u32[]{:S(2)}, u32[]{:S(2)}) collective-permute-start(f32[6,256]{1,0:T(8,128)} %bitcast.568), channel_id=1, source_target_pairs={{3,0},{0,1},{1,2},{2,3},{7,4},{4,5},{5,6},{6,7},{11,8},{8,9},{9,10... | collective-permute-start | bytes 18440 | tf_op jit(solution)/shard_map/ppermute | solution.py:23
  232.4 846.0 %collective-permute-start.1 = (f32[6,256]{1,0:T(8,128)}, f32[6,256]{1,0:T(8,128)}, u32[]{:S(2)}, u32[]{:S(2)}) collective-permute-start(f32[6,256]{1,0:T(8,128)} %bitcast.566), channel_id=1, source_target_pairs={{4,0},{8,4},{12,8},{16,12},{20,16},{24,20},{28,24},{32,28},{36,32}... | collective-permute-start | bytes 18440 | tf_op jit(solution)/shard_map/ppermute | solution.py:17
  238.3 840.1 %collective-permute-start = (f32[6,256]{1,0:T(8,128)}, f32[6,256]{1,0:T(8,128)}, u32[]{:S(2)}, u32[]{:S(2)}) collective-permute-start(f32[6,256]{1,0:T(8,128)} %bitcast.564), channel_id=1, source_target_pairs={{0,4},{4,8},{8,12},{12,16},{16,20},{20,24},{24,28},{28,32},{32,36}... | collective-permute-start | bytes 18440 | tf_op jit(solution)/shard_map/ppermute | solution.py:17
  437.7 219.0 %copy-start.8 = (f32[3,32,128]{2,1,0:T(8,128)}, f32[3,32,128]{2,1,0:T(8,128)S(1)}, u32[]{:S(2)}) copy-start(f32[3,32,128]{2,1,0:T(8,128)S(1)} %get-tuple-element.164) | copy-start | bytes 147460
  696.4 5.4 copy-start.24
  696.4 53.9 %all-to-all-start.1 = ((f32[4,128,8,128]{3,2,0,1:T(8,128)}), f32[4,128,8,128]{3,2,0,1:T(8,128)}, u32[]{:S(2)}, u32[]{:S(2)}) async-start(f32[4,128,8,128]{3,2,0,1:T(8,128)} %copy.117), calls=%async_computation.1 | async-start | bytes 4194304 | tf_op jit(solution)/shard_map/all_to_all | solution.py:131
  757.6 2.2 copy-start.6
  759.4 1.6 copy-start.1
  761.0 3.5 copy-start.14
  789.3 232.7 %all-to-all-start.2 = ((f32[4,1,131072]{2,1,0:T(1,128)}), f32[4,1,131072]{2,1,0:T(1,128)}, u32[]{:S(2)}, u32[]{:S(2)}) async-start(f32[4,1,131072]{2,1,0:T(1,128)} %reshape.572), calls=%async_computation.2 | async-start | bytes 4194304 | tf_op jit(solution)/shard_map/all_to_all | solution.py:133
  961.8 51.3 %copy-start.15 = (f32[1,128]{1,0:T(1,128)S(1)}, f32[1,128]{1,0:T(1,128)}, u32[]{:S(2)}) copy-start(f32[1,128]{1,0:T(1,128)} %get-tuple-element.299) | copy-start | bytes 1540
  961.8 51.3 %copy-start.16 = (f32[1,128]{1,0:T(1,128)S(1)}, f32[1,128]{1,0:T(1,128)}, u32[]{:S(2)}) copy-start(f32[1,128]{1,0:T(1,128)} %get-tuple-element.301) | copy-start | bytes 1540
  961.8 51.3 %copy-start.17 = (f32[1,128]{1,0:T(1,128)S(1)}, f32[1,128]{1,0:T(1,128)}, u32[]{:S(2)}) copy-start(f32[1,128]{1,0:T(1,128)} %get-tuple-element.303) | copy-start | bytes 1540
  961.8 51.3 %copy-start.18 = (f32[1,128]{1,0:T(1,128)S(1)}, f32[1,128]{1,0:T(1,128)}, u32[]{:S(2)}) copy-start(f32[1,128]{1,0:T(1,128)} %get-tuple-element.305) | copy-start | bytes 1540
  961.8 51.3 %copy-start.19 = (f32[1,128]{1,0:T(1,128)S(1)}, f32[1,128]{1,0:T(1,128)}, u32[]{:S(2)}) copy-start(f32[1,128]{1,0:T(1,128)} %get-tuple-element.307) | copy-start | bytes 1540
  961.8 51.3 %copy-start.20 = (f32[1,128]{1,0:T(1,128)S(1)}, f32[1,128]{1,0:T(1,128)}, u32[]{:S(2)}) copy-start(f32[1,128]{1,0:T(1,128)} %get-tuple-element.309) | copy-start | bytes 1540
  961.8 51.3 %copy-start.21 = (f32[1,128]{1,0:T(1,128)S(1)}, f32[1,128]{1,0:T(1,128)}, u32[]{:S(2)}) copy-start(f32[1,128]{1,0:T(1,128)} %get-tuple-element.311) | copy-start | bytes 1540
  961.8 51.3 %copy-start.22 = (f32[1,128]{1,0:T(1,128)S(1)}, f32[1,128]{1,0:T(1,128)}, u32[]{:S(2)}) copy-start(f32[1,128]{1,0:T(1,128)} %get-tuple-element.313) | copy-start | bytes 1540
  961.8 51.3 %copy-start.23 = (f32[1,128]{1,0:T(1,128)S(1)}, f32[1,128]{1,0:T(1,128)}, u32[]{:S(2)}) copy-start(f32[1,128]{1,0:T(1,128)} %get-tuple-element.315) | copy-start | bytes 1540
  1014.0 1.4 copy-start.3
  1052.6 11.0 %copy-start.4 = (f32[512,512]{1,0:T(8,128)S(1)}, f32[512,512]{1,0:T(8,128)}, u32[]{:S(2)}) copy-start(f32[512,512]{1,0:T(8,128)} %copy-done.3) | copy-start | bytes 3145732
  1052.6 11.0 %copy-start.5 = (f32[128,512]{1,0:T(8,128)S(1)}, f32[128,512]{1,0:T(8,128)}, u32[]{:S(2)}) copy-start(f32[128,512]{1,0:T(8,128)} %fusion.238) | copy-start | bytes 786436
  1052.6 11.4 %copy-start.7 = (f32[4,128,128]{1,2,0:T(8,128)S(1)}, f32[4,128,128]{1,2,0:T(8,128)}, u32[]{:S(2)}) copy-start(f32[4,128,128]{1,2,0:T(8,128)} %custom-call.37) | copy-start | bytes 786436
  1052.6 39.6 %all-to-all-start.3 = ((f32[4,128,8,128]{3,2,0,1:T(8,128)}), f32[4,128,8,128]{3,2,0,1:T(8,128)}, u32[]{:S(2)}, u32[]{:S(2)}) async-start(f32[4,128,8,128]{3,2,0,1:T(8,128)} %copy.124), calls=%async_computation.3 | async-start | bytes 4194304 | tf_op jit(solution)/shard_map/all_to_all | solution.py:136
  1067.6 2.9 copy-start
  1074.2 3.7 copy-start.2
where the time goes:
time: 1110 us; the launch traced here: 1100 us
  other arithmetic  505 us (45%)
  local copies, waits for them, and re-layouts  281 us (25%)
  loops' own time  125 us (11%)
  waiting for transfers between devices  50.7 us (5%)
  matrix products  47.3 us (4%)
  between operations  44 us (4%)
  starting transfers between devices  42.7 us (4%)
    scatter-add x3, other arithmetic, on_device(): deposit = jnp.zeros_like(flat_speed).at[:, cell_index].add(force).reshape...  129 us
    another operation x2, loops' own time, wall_compact(): lax.linalg.tridiagonal_solve(lower, middle, upper, rhs.astype(jnp.float32))  125 us
    gather x2, local copies, waits for them, and re-layouts, on_device(): fluid = jnp.take(flat_speed, cell_index, axis=1)  121 us
    div x4, other arithmetic, wall_compact(): lax.linalg.tridiagonal_solve(lower, middle, upper, rhs.astype(jnp.float32))  80.3 us
    another operation x14, other arithmetic, periodic_compact(): factor = jnp.linalg.cholesky(lhs.astype(jnp.float32))  78.7 us
    sub x3, other arithmetic, wall_compact(): lax.linalg.tridiagonal_solve(lower, middle, upper, rhs.astype(jnp.float32))  61 us
    scatter-add x1, other arithmetic, on_device(): outgoing = jnp.zeros((6, 4 * MIG + 1), jnp.float32).at[:, target].add(jnp...  53.6 us
    another operation x15, local copies, waits for them, and re-layouts  46.3 us
  transfers between devices with their start and end apart: 8, of which 2 were waited for; matrix products, arithmetic and copies ran while one was open for 75% of the time, Pallas kernels for 0%

commit v1 on v0

--- a/solution.py
+++ b/solution.py
@@ -130,8 +130,9 @@
     partial_y = -normal_pencil[1] * along_y + viscous * curve_y
     span_pencil = lax.all_to_all(normal_pencil, "col", split_axis=1, concat_axis=3, tiled=True)
     partial_z = spanwise_terms(span_pencil, viscous)
-    partial_y = partial_y + lax.all_to_all(
-        partial_z, "col", split_axis=3, concat_axis=1, tiled=True
+    partial_y = partial_y + jnp.concatenate(
+        lax.all_to_all(jnp.stack(jnp.split(partial_z, lax.axis_size("col"), axis=3)), "col", 0, 0),
+        axis=1,
     )
     tendency = partial_x + lax.all_to_all(partial_y, "row", split_axis=1, concat_axis=2, tiled=True)
     staying = live & (destination == 0)

time: 1110 us -> 1070 us (0.964)
  local copies, waits for them, and re-layouts: 281 us -> 254 us
    unnamed x58 -> x60, local copies, waits for them, and re-layouts: 24.1 us -> 9.41 us
    another operation x15 -> x16, local copies, waits for them, and re-layouts: 46.3 us -> 47.2 us
  transfers between devices with their start and end apart: 8 -> 8, of which waited for: 2 -> 2; matrix products, arithmetic and copies ran while one was open for 75% -> 74% of each run, Pallas kernels for 0% -> 0%
where the time goes in v1:
time: 1070 us; the launch traced here: 1060 us
  other arithmetic  498 us (47%)
  local copies, waits for them, and re-layouts  254 us (24%)
  loops' own time  124 us (12%)
  waiting for transfers between devices  50.3 us (5%)
  between operations  44.3 us (4%)
  matrix products  44 us (4%)
  starting transfers between devices  41.1 us (4%)
    scatter-add x3, other arithmetic, on_device(): deposit = jnp.zeros_like(flat_speed).at[:, cell_index].add(force).reshape...  128 us
    another operation x2, loops' own time, wall_compact(): lax.linalg.tridiagonal_solve(lower, middle, upper, rhs.astype(jnp.float32))  124 us
    gather x2, local copies, waits for them, and re-layouts, on_device(): fluid = jnp.take(flat_speed, cell_index, axis=1)  121 us
    div x4, other arithmetic, wall_compact(): lax.linalg.tridiagonal_solve(lower, middle, upper, rhs.astype(jnp.float32))  79.8 us
    another operation x14, other arithmetic, periodic_compact(): factor = jnp.linalg.cholesky(lhs.astype(jnp.float32))  79 us
    sub x3, other arithmetic, wall_compact(): lax.linalg.tridiagonal_solve(lower, middle, upper, rhs.astype(jnp.float32))  61 us
    scatter-add x1, other arithmetic, on_device(): outgoing = jnp.zeros((6, 4 * MIG + 1), jnp.float32).at[:, target].add(jnp...  53.6 us
    another operation x15, local copies, waits for them, and re-layouts  47 us
  transfers between devices with their start and end apart: 8, of which 2 were waited for; matrix products, arithmetic and copies ran while one was open for 74% of the time, Pallas kernels for 0%

profile of v1, /device:TPU:1, one launch (start us, length us, event | category | flops | bytes accessed | tf_op | source)
XLA Modules:
  0.0 1055.3 jit_solution(10082964858229339219)
XLA Ops:
  0.6 4.3 copy.112
  4.9 10.5 all-to-all-start
  16.9 30.5 %copy.108 = f32[3,2,512,128]{0,3,2,1:T(8,128)} copy(f32[3,2,512,128]{3,2,1,0:T(8,128)S(1)} %slice-done) | data formatting | bytes 3145728 | tf_op jit(solution)/shard_map/slice | solution.py:111
  47.4 118.6 %gather_fusion = f32[8192,3]{1,0:T(8,128)} fusion(f32[3,131072]{0,1:T(8,128)} %bitcast.277, s32[8192]{0:T(1024)S(1)} %get-tuple-element.484), kind=kCustom, calls=%fused_computation | custom fusion | bytes 229376 | tf_op jit(solution)/shard_map/jit(_take)/gather | solution.py:112
  166.0 2.9 copy.109
  170.5 2.7 copy.122
  173.2 53.6 %scatter_custom_fusion.1 = f32[6,1025]{0,1:T(8,128)S(1)} fusion(s32[8192]{0:T(1024)S(1)} %compare_select_fusion, f32[8192,6]{1,0:T(8,128)} %copy.122, f32[]{:T(128)} %constant.319.clone.1), kind=kCustom, calls=%fused_computation.322 | custom fusion | flops 49152 | bytes 25112 | tf_op jit(solution)/shard_map/scatter-add | solution.py:145
  227.0 4.1 collective-permute-start.3
  232.5 5.3 collective-permute-start.1
  242.8 193.3 %while.34 = (s32[]{:T(128)}, f32[]{:T(128)}, f32[128]{0:T(128)S(1)}, f32[3,32]{1,0:T(4,128)S(1)}, f32[3,32,128]{2,1,0:T(8,128)S(1)}, /*index=5*/f32[3,32]{1,0:T(...) while((s32[]{:T(128)}, f32[]{:T(128)}, ...), condition=%wide.region_10.11_spmd, body=%wide.region_9.10_spmd.sunk | while | flops 12417 | bytes 103669 | solution.py:75
  286.3 20.1 %fusion.526 = (f32[128]{0:T(128)S(1)}, f32[128]{0:T(128)S(1)}, f32[128]{0:T(128)S(1)}, f32[128]{0:T(128)S(1)}, f32[128]{0:T(128)S(1)}, /*index=5*/f32[128]{0:T(1...) fusion(f32[3,32,128]{2,1,0:T(8,128)S(1)} %get-tuple-element.112, ...), kind=kLoop, calls=%fused_computation.44.clone.1 | loop fusion | flops 12288 | bytes 33664 | tf_op jit(solution)/shard_map/while/body/eval_jaxpr/div | solution.py:75
  350.7 20.1 %fusion.526 = (f32[128]{0:T(128)S(1)}, f32[128]{0:T(128)S(1)}, f32[128]{0:T(128)S(1)}, f32[128]{0:T(128)S(1)}, f32[128]{0:T(128)S(1)}, /*index=5*/f32[128]{0:T(1...) fusion(f32[3,32,128]{2,1,0:T(8,128)S(1)} %get-tuple-element.112, ...), kind=kLoop, calls=%fused_computation.44.clone.1 | loop fusion | flops 12288 | bytes 33664 | tf_op jit(solution)/shard_map/while/body/eval_jaxpr/div | solution.py:75
  415.0 20.1 %fusion.526 = (f32[128]{0:T(128)S(1)}, f32[128]{0:T(128)S(1)}, f32[128]{0:T(128)S(1)}, f32[128]{0:T(128)S(1)}, f32[128]{0:T(128)S(1)}, /*index=5*/f32[128]{0:T(1...) fusion(f32[3,32,128]{2,1,0:T(8,128)S(1)} %get-tuple-element.112, ...), kind=kLoop, calls=%fused_computation.44.clone.1 | loop fusion | flops 12288 | bytes 33664 | tf_op jit(solution)/shard_map/while/body/eval_jaxpr/div | solution.py:75
  439.8 11.7 %cholesky.104 = f32[128,128]{1,0:T(8,128)S(1)} custom-call(f32[128,128]{1,0:T(8,128)S(1)} %cholesky.266), custom_call_target="Cholesky" | custom-call | tf_op jit(solution)/shard_map/jit(cholesky)/cholesky | solution.py:38
  451.7 9.8 custom-call.34
  462.2 11.7 %cholesky.217 = f32[128,128]{1,0:T(8,128)S(1)} custom-call(f32[128,128]{1,0:T(8,128)S(1)} %cholesky.270), custom_call_target="Cholesky" | custom-call | tf_op jit(solution)/shard_map/jit(cholesky)/cholesky | solution.py:38
  473.9 10.3 custom-call.35
  484.8 11.7 %cholesky.238 = f32[128,128]{1,0:T(8,128)S(1)} custom-call(f32[128,128]{1,0:T(8,128)S(1)} %cholesky.275), custom_call_target="Cholesky" | custom-call | tf_op jit(solution)/shard_map/jit(cholesky)/cholesky | solution.py:38
  496.6 9.8 custom-call.36
  507.0 11.7 %cholesky.255 = f32[128,128]{1,0:T(8,128)S(1)} custom-call(f32[128,128]{1,0:T(8,128)S(1)} %convolution_subtract_fusion.8), custom_call_target="Cholesky" | custom-call | tf_op jit(solution)/shard_map/jit(cholesky)/cholesky | solution.py:38
  559.2 19.5 %fusion.304 = (f32[128]{0:T(128)S(1)}, f32[128]{0:T(128)S(1)}, f32[128]{0:T(128)S(1)}, f32[128]{0:T(128)S(1)}, f32[128]{0:T(128)S(1)}, /*index=5*/f32[128]{0:T(1...) fusion(f32[128,128]{1,0:T(8,128)S(1)} %select_select_fusion.1, ...), kind=kLoop, calls=%fused_computation.493 | loop fusion | flops 11904 | bytes 32504 | tf_op jit(solution)/shard_map/eval_jaxpr/div | solution.py:75
  583.2 6.6 sort
  589.7 65.7 %while.35 = (s32[]{:T(128)}, f32[128]{0:T(128)S(1)}, f32[3,32,128]{2,1,0:T(8,128)S(1)}, f32[3,32,128]{2,1,0:T(8,128)S(1)}, f32[3,32]{1,0:T(4,128)S(1)}, /*index=...) while((s32[]{:T(128)}, f32[128]{0:T(128)S(1)}, ...), condition=%wide.region_12.13_spmd, body=%wide.region_11.12_spmd.sunk | while | flops 8226 | bytes 101341 | solution.py:75
  591.2 20.3 %fusion.529 = (f32[128]{0:T(128)S(1)}, f32[128]{0:T(128)S(1)}, f32[128]{0:T(128)S(1)}, f32[128]{0:T(128)S(1)}, f32[128]{0:T(128)S(1)}, /*index=5*/f32[128]{0:T(1...) fusion(f32[3,32,128]{2,1,0:T(8,128)S(1)} %get-tuple-element.124, ...), kind=kLoop, calls=%fused_computation.172.clone.1 | loop fusion | flops 8192 | bytes 33536 | tf_op jit(solution)/shard_map/while/body/eval_jaxpr/sub | solution.py:75
  613.1 20.3 %fusion.529 = (f32[128]{0:T(128)S(1)}, f32[128]{0:T(128)S(1)}, f32[128]{0:T(128)S(1)}, f32[128]{0:T(128)S(1)}, f32[128]{0:T(128)S(1)}, /*index=5*/f32[128]{0:T(1...) fusion(f32[3,32,128]{2,1,0:T(8,128)S(1)} %get-tuple-element.124, ...), kind=kLoop, calls=%fused_computation.172.clone.1 | loop fusion | flops 8192 | bytes 33536 | tf_op jit(solution)/shard_map/while/body/eval_jaxpr/sub | solution.py:75
  635.0 20.3 %fusion.529 = (f32[128]{0:T(128)S(1)}, f32[128]{0:T(128)S(1)}, f32[128]{0:T(128)S(1)}, f32[128]{0:T(128)S(1)}, f32[128]{0:T(128)S(1)}, /*index=5*/f32[128]{0:T(1...) fusion(f32[3,32,128]{2,1,0:T(8,128)S(1)} %get-tuple-element.124, ...), kind=kLoop, calls=%fused_computation.172.clone.1 | loop fusion | flops 8192 | bytes 33536 | tf_op jit(solution)/shard_map/while/body/eval_jaxpr/sub | solution.py:75
  657.1 3.2 fusion.368
  660.4 3.3 fusion.367
  663.7 3.0 fusion.366
  666.7 3.4 fusion.365
  670.1 3.3 fusion.364
  673.4 3.3 fusion.363
  676.7 3.1 fusion.362
  679.7 3.2 fusion.361
  682.9 7.0 convolution_bitcast_fusion
  690.1 2.7 copy.144
  692.7 2.5 copy.114
  695.3 5.3 all-to-all-start.1
  700.5 10.8 %while.36 = (s32[]{:T(128)}, f32[512,512]{1,0:T(8,128)S(1)}, s32[4,2]{0,1:T(2,128)S(1)}, f32[4,128,128]{2,1,0:T(8,128)}, s32[]{:T(128)}) while((s32[]{:T(128)}, f32[512,512]{1,0:T(8,128)S(1)}, s32[4,2]{0,1:T(2,128)S(1)}, f32[4,128,128]{2,1,0:T(8,128)}, s32[]{:T(128)}) %tuple.402), condition=%wide.while_cond.1, body=%wide.while_body.1.sunk | while | flops 2 | bytes 132205 | solution.py:39
  706.6 2.0 bitcast_dynamic-update-slice_fusion.8
  711.4 37.8 %all-to-all-done.1 = f32[4,128,8,128]{3,2,0,1:T(8,128)} async-done(((f32[4,128,8,128]{3,2,0,1:T(8,128)}), f32[4,128,8,128]{3,2,0,1:T(8,128)}, u32[]{:S(2)}, u32[]{:S(2)}) %all-to-all-start.1) | async-done | bytes 2097184 | tf_op jit(solution)/shard_map/all_to_all | solution.py:131
  749.1 4.3 copy.118
  753.4 3.3 all_to_all.49
  760.1 3.5 fusion.493
  763.6 7.9 bitcast_add_fusion.2
  773.8 4.4 all-to-all-start.2
  778.2 2.7 fusion.360
  780.9 40.7 %custom-call.37 = f32[4,128,128]{1,2,0:T(8,128)} custom-call(f32[4,128,128]{2,1,0:T(8,128)} %get-tuple-element.177), custom_call_target="InvertDiagBlocksLowerTriangular" | custom-call | tf_op jit(solution)/shard_map/jit(_cho_solve)/triangular_solve | solution.py:39
  821.7 2.7 copy.110
  824.3 121.7 %scatter_custom_fusion = f32[3,131072]{0,1:T(8,128)} fusion(s32[8192]{0:T(1024)} %get-tuple-element.196, f32[]{:T(128)} %constant.319.clone.1, f32[8192,3]{1,0:T(8,128)} %copy.110, s32[8192]{0:T(1024)S(1)} %broadcast_clamp_fusion), kind=kCustom, calls=%fused_computation.235 | custom fusion | flops 24576 | bytes 1573376 | tf_op jit(solution)/shard_map/scatter-add | solution.py:121
  946.0 36.2 %copy.134 = f32[3,2,512,128]{3,2,1,0:T(8,128)} copy(f32[3,2,512,128]{0,3,2,1:T(8,128)} %bitcast.280) | data formatting | bytes 3145728 | tf_op jit(solution)/shard_map/reshape.86
  982.2 2.6 fusion.359
  984.8 2.6 fusion.358
  987.4 2.7 fusion.357
  990.0 2.6 fusion.356
  992.6 2.6 fusion.355
  1002.9 3.3 fusion.226
  1008.5 2.4 bitcast_add_fusion.1
  1010.8 2.5 copy.120
  1013.4 9.7 all-to-all-start.3
  1030.0 3.6 fusion.492
  1033.6 3.7 bitcast_add_fusion.3
  1039.2 12.5 %all-to-all-done.3 = f32[4,128,8,128]{3,2,0,1:T(8,128)} async-done(((f32[4,128,8,128]{3,2,0,1:T(8,128)}), f32[4,128,8,128]{3,2,0,1:T(8,128)}, u32[]{:S(2)}, u32[]{:S(2)}) %all-to-all-start.3) | async-done | bytes 2097184 | tf_op jit(solution)/shard_map/all_to_all | solution.py:137
  1051.7 3.1 bitcast_add_fusion
  (217 shorter events, 66.6 us)
Async XLA Ops:
  4.9 685.2 %all-to-all-start = ((f32[4,2,512,128]{3,0,1,2:T(4,128)}), f32[4,2,512,128]{3,0,1,2:T(4,128)}, u32[]{:S(2)}, u32[]{:S(2)}) async-start(f32[4,2,512,128]{3,0,1,2:T(4,128)} %copy.112), calls=%async_computation | async-start | bytes 4194304 | tf_op jit(solution)/shard_map/all_to_all | solution.py:125
  15.4 0.8 copy-start.12
  15.4 1.4 slice-start
  166.0 3.6 copy-start.13
  166.0 3.6 copy-start.11
  166.0 3.6 copy-start.14
  170.5 2.7 copy-start.15
  227.0 810.8 %collective-permute-start.3 = (f32[6,256]{1,0:T(8,128)S(1)}, f32[6,256]{1,0:T(8,128)}, u32[]{:S(2)}, u32[]{:S(2)}) collective-permute-start(f32[6,256]{1,0:T(8,128)S(1)} %bitcast.1866), channel_id=1, source_target_pairs={{1,0},{2,1},{3,2},{0,3},{5,4},{6,5},{7,6},{4,7},{9,8},{10,9},{11,1... | collective-permute-start | bytes 18440 | tf_op jit(solution)/shard_map/ppermute | solution.py:23
  231.8 806.0 %collective-permute-start.2 = (f32[6,256]{1,0:T(8,128)}, f32[6,256]{1,0:T(8,128)}, u32[]{:S(2)}, u32[]{:S(2)}) collective-permute-start(f32[6,256]{1,0:T(8,128)} %bitcast.571), channel_id=1, source_target_pairs={{3,0},{0,1},{1,2},{2,3},{7,4},{4,5},{5,6},{6,7},{11,8},{8,9},{9,10... | collective-permute-start | bytes 18440 | tf_op jit(solution)/shard_map/ppermute | solution.py:23
  232.5 805.3 %collective-permute-start.1 = (f32[6,256]{1,0:T(8,128)}, f32[6,256]{1,0:T(8,128)}, u32[]{:S(2)}, u32[]{:S(2)}) collective-permute-start(f32[6,256]{1,0:T(8,128)} %bitcast.569), channel_id=1, source_target_pairs={{4,0},{8,4},{12,8},{16,12},{20,16},{24,20},{28,24},{32,28},{36,32}... | collective-permute-start | bytes 18440 | tf_op jit(solution)/shard_map/ppermute | solution.py:17
  238.4 799.4 %collective-permute-start = (f32[6,256]{1,0:T(8,128)}, f32[6,256]{1,0:T(8,128)}, u32[]{:S(2)}, u32[]{:S(2)}) collective-permute-start(f32[6,256]{1,0:T(8,128)} %bitcast.567), channel_id=1, source_target_pairs={{0,4},{4,8},{8,12},{12,16},{16,20},{20,24},{24,28},{28,32},{32,36}... | collective-permute-start | bytes 18440 | tf_op jit(solution)/shard_map/ppermute | solution.py:17
  436.1 219.3 %copy-start.10 = (f32[3,32,128]{2,1,0:T(8,128)}, f32[3,32,128]{2,1,0:T(8,128)S(1)}, u32[]{:S(2)}) copy-start(f32[3,32,128]{2,1,0:T(8,128)S(1)} %get-tuple-element.164) | copy-start | bytes 147460
  695.3 5.3 copy-start.26
  695.3 53.8 %all-to-all-start.1 = ((f32[4,128,8,128]{3,2,0,1:T(8,128)}), f32[4,128,8,128]{3,2,0,1:T(8,128)}, u32[]{:S(2)}, u32[]{:S(2)}) async-start(f32[4,128,8,128]{3,2,0,1:T(8,128)} %copy.114), calls=%async_computation.1 | async-start | bytes 4194304 | tf_op jit(solution)/shard_map/all_to_all | solution.py:131
  756.6 2.2 copy-start.8
  758.5 1.6 copy-start.1
  760.1 3.5 copy-start.16
  773.8 232.4 %all-to-all-start.2 = ((f32[4,4,32,8,128]{4,2,3,1,0:T(8,128)}), f32[4,4,32,8,128]{4,2,3,1,0:T(8,128)}, u32[]{:S(2)}, u32[]{:S(2)}) async-start(f32[4,4,32,8,128]{4,2,3,1,0:T(8,128)} %pad_maximum_fusion), calls=%async_computation.2 | async-start | bytes 4194304 | tf_op jit(solution)/shard_map/all_to_all | solution.py:134
  946.0 51.2 %copy-start.17 = (f32[1,128]{1,0:T(1,128)S(1)}, f32[1,128]{1,0:T(1,128)}, u32[]{:S(2)}) copy-start(f32[1,128]{1,0:T(1,128)} %get-tuple-element.299) | copy-start | bytes 1540
  946.0 51.2 %copy-start.18 = (f32[1,128]{1,0:T(1,128)S(1)}, f32[1,128]{1,0:T(1,128)}, u32[]{:S(2)}) copy-start(f32[1,128]{1,0:T(1,128)} %get-tuple-element.301) | copy-start | bytes 1540
  946.0 51.2 %copy-start.19 = (f32[1,128]{1,0:T(1,128)S(1)}, f32[1,128]{1,0:T(1,128)}, u32[]{:S(2)}) copy-start(f32[1,128]{1,0:T(1,128)} %get-tuple-element.303) | copy-start | bytes 1540
  946.0 51.2 %copy-start.20 = (f32[1,128]{1,0:T(1,128)S(1)}, f32[1,128]{1,0:T(1,128)}, u32[]{:S(2)}) copy-start(f32[1,128]{1,0:T(1,128)} %get-tuple-element.305) | copy-start | bytes 1540
  946.0 51.2 %copy-start.21 = (f32[1,128]{1,0:T(1,128)S(1)}, f32[1,128]{1,0:T(1,128)}, u32[]{:S(2)}) copy-start(f32[1,128]{1,0:T(1,128)} %get-tuple-element.307) | copy-start | bytes 1540
  946.0 51.2 %copy-start.22 = (f32[1,128]{1,0:T(1,128)S(1)}, f32[1,128]{1,0:T(1,128)}, u32[]{:S(2)}) copy-start(f32[1,128]{1,0:T(1,128)} %get-tuple-element.309) | copy-start | bytes 1540
  946.0 51.2 %copy-start.23 = (f32[1,128]{1,0:T(1,128)S(1)}, f32[1,128]{1,0:T(1,128)}, u32[]{:S(2)}) copy-start(f32[1,128]{1,0:T(1,128)} %get-tuple-element.311) | copy-start | bytes 1540
  946.0 51.2 %copy-start.24 = (f32[1,128]{1,0:T(1,128)S(1)}, f32[1,128]{1,0:T(1,128)}, u32[]{:S(2)}) copy-start(f32[1,128]{1,0:T(1,128)} %get-tuple-element.313) | copy-start | bytes 1540
  946.0 51.2 %copy-start.25 = (f32[1,128]{1,0:T(1,128)S(1)}, f32[1,128]{1,0:T(1,128)}, u32[]{:S(2)}) copy-start(f32[1,128]{1,0:T(1,128)} %get-tuple-element.315) | copy-start | bytes 1540
  998.1 1.4 copy-start.4
  1006.2 2.2 copy-start.2
  1006.2 2.3 copy-start.7
  1013.4 9.7 copy-start.5
  1013.4 9.7 copy-start.6
  1013.4 10.1 copy-start.9
  1013.4 38.3 %all-to-all-start.3 = ((f32[4,128,8,128]{3,2,0,1:T(8,128)}), f32[4,128,8,128]{3,2,0,1:T(8,128)}, u32[]{:S(2)}, u32[]{:S(2)}) async-start(f32[4,128,8,128]{3,2,0,1:T(8,128)} %copy.120), calls=%async_computation.3 | async-start | bytes 4194304 | tf_op jit(solution)/shard_map/all_to_all | solution.py:137
  1027.0 2.9 copy-start
  1033.6 3.7 copy-start.3
